TPU v7x, 128 devices: a whole 4x4x4 slice. The times are simulated.
128 devices in a mesh: rows: 16 (over z, x), sub: 8 (over y, core).
Axes of the slice: x: 4, y: 4, z: 4, core: 2. Of those that a mesh axis runs over, the one named last changes fastest.
Arguments:
- residuals: bfloat16 [65536, 1024], P(('rows', 'sub')), may hold values from -14 to 14
- codes: int32 [65536, 64], P(('rows', 'sub')), may hold values from 0 to 255, as said below
- codebook: bfloat16 [64, 16, 256], replicated, may hold values from -4 to 4
Outputs:
- rotated: bfloat16 [65536, 1024], P(('rows', 'sub'))
- new_codebook: float32 [64, 16, 256], P('sub', None, 'rows')
Inputs may be any that keep to these rules, and one draw needn't show every extreme that they name: `codes`: every codeword 0 to 255 occurs in every column.
All inputs are finite; a program needn't handle non-finite values.
Results may differ from a plain program's by a relative error of at most 0.0042.
Values may be sent and summed in bfloat16 or wider, within the bound.
A program may use at most 64 MiB of HBM per device.

v0:
```python
import jax
import jax.numpy as jnp
from jax import lax
from jax.sharding import PartitionSpec as P

D = 1024
SUBS = 64
CODES = 256
ITERS = 2


def rebuild(labels, codebook):
    rows = labels.shape[0]
    block = min(rows, 16384 // SUBS)
    levels = jnp.arange(CODES).astype(jnp.bfloat16)

    def one_block(piece):
        hot = (piece[:, :, None] == levels[None, None, :]).astype(jnp.bfloat16)
        rec = jnp.einsum("rmk,mdk->rmd", hot, codebook, preferred_element_type=jnp.float32)
        return rec.astype(jnp.bfloat16).reshape(block, D)

    return lax.map(one_block, labels.reshape(rows // block, block, SUBS)).reshape(rows, D)


def tally(values, labels, count):
    rows = values.shape[0]
    width = values.shape[1] // count
    block = min(rows, 16384 // count)
    levels = jnp.arange(CODES).astype(jnp.bfloat16)

    def one_step(index, carry):
        sums, totals = carry
        vals = lax.dynamic_slice_in_dim(values, index * block, block, 0).reshape(
            block, count, width
        )
        labs = lax.dynamic_slice_in_dim(labels, index * block, block, 0)
        hot = (labs[:, :, None] == levels[None, None, :]).astype(jnp.bfloat16)
        sums = sums + jnp.einsum("rmd,rmk->mdk", vals, hot, preferred_element_type=jnp.float32)
        totals = totals + jnp.sum(hot, axis=0, dtype=jnp.float32)
        return (sums, totals)

    start = (jnp.zeros((count, width, CODES), jnp.float32), jnp.zeros((count, CODES), jnp.float32))
    return lax.fori_loop(0, rows // block, one_step, start)


def iterate(polar, gram, make_gram):
    highest = lax.Precision.HIGHEST
    scale = jnp.sqrt(jnp.sqrt(jnp.sum(gram * gram) + 1e-06))
    polar = polar / scale
    gram = gram / (scale * scale)
    for step in range(ITERS):
        if step > 0:
            gram = make_gram(polar)
        moved = jnp.dot(polar, gram, precision=highest)
        polar = 3.4445 * polar - 4.775 * moved + 2.0315 * jnp.dot(moved, gram, precision=highest)
    return polar


def per_device(residuals, codes, codebook):
    labels = codes.astype(jnp.bfloat16)
    recon = rebuild(labels, codebook)
    highest = lax.Precision.HIGHEST
    contract = (((0,), (0,)), ((), ()))
    local = lax.dot_general(residuals, recon, contract, preferred_element_type=jnp.float32)
    cross = lax.psum(local, ("rows", "sub"))
    polar = cross / jnp.sqrt(jnp.sum(cross * cross) + 1e-06)

    def local_gram(current):
        return lax.dot_general(current, current, contract, precision=highest)

    polar = iterate(polar, local_gram(polar), local_gram)
    rotation = polar.astype(jnp.bfloat16)
    rotated = jnp.dot(residuals, rotation, preferred_element_type=jnp.float32).astype(jnp.bfloat16)
    owned_rows, owned_labels = (
        lax.all_to_all(rotated, "sub", split_axis=1, concat_axis=0, tiled=True),
        lax.all_to_all(labels, "sub", split_axis=1, concat_axis=0, tiled=True),
    )
    sums, totals = tally(owned_rows, owned_labels, owned_labels.shape[1])
    sums, totals = (
        lax.psum_scatter(sums, "rows", scatter_dimension=2, tiled=True),
        lax.psum_scatter(totals[:, None, :], "rows", scatter_dimension=2, tiled=True),
    )
    return (rotated, sums / totals)


def solution(mesh):
    return jax.shard_map(
        per_device,
        mesh=mesh,
        in_specs=(P(("rows", "sub"), None), P(("rows", "sub"), None), P()),
        out_specs=(P(("rows", "sub"), None), P("sub", None, "rows")),
        check_vma=False,
    )
```

profile of v0, /device:TPU:0, one launch (start us, length us, event | category | flops | bytes accessed | tf_op | source)
XLA Modules:
  0.0 439.1 jit_solution(3394257541561877917)
XLA Ops:
  7.2 0.0 copy-start
  7.2 0.0 all-reduce.5.cloned.1.call-start
  7.2 1.0 convert_element_type.39
  8.2 8.8 %while.27 = (s32[]{:T(128)}, bf16[2,256,1024]{2,1,0:T(8,128)(2,1)S(1)}, bf16[2,256,64]{1,2,0:T(8,128)(2,1)S(1)}, bf16[64,16,256]{2,1,0:T(8,128)(2,1)}, s32[]{:T(128)}) while((s32[]{:T(128)}, bf16[2,256,1024]{2,1,0:T(8,128)(2,1)S(1)}, bf16[2,256,64]{1,2,0:T(8,128)(2,1)S(1)}, bf16[64,16,256]{2,1,0:T(8,128)(2,1)}, s32[]{:T(128)}) %tuple.70), condition=%wide.region_1.2_spmd.clone, body=%wide.region_0.1_spmd.clone.sunk | while | flops 138674432 | bytes 3245125 | solution.py:22
  8.3 4.1 fusion.45
  12.4 0.2 copy.38
  12.7 4.1 fusion.45
  16.8 0.2 copy.38
  17.1 0.0 copy-done
  17.1 3.3 convolution_bitcast_fusion
  20.3 0.0 all-reduce.5.cloned.1.call-update
  20.3 156.7 %all-reduce.5.cloned.1.call-done = f32[1024,1024]{0,1:T(8,128)} async-done(((f32[1024,1024]{0,1:T(8,128)}), f32[1024,1024]{0,1:T(8,128)}) %all-reduce.5.cloned.1.call-update) | async-done | bytes 4194320 | tf_op jit(solution)/shard_map/psum | solution.py:65
  177.0 3.9 multiply_reduce_fusion.1
  181.6 19.1 %multiply_reduce_fusion = (f32[]{:T(128)}, f32[1024,1024]{1,0:T(8,128)}) fusion(f32[1024,1024]{0,1:T(8,128)} %all-reduce.5.cloned.1.call-done, f32[]{:T(128)S(6)} %sqrt.9), kind=kOutput, calls=%fused_computation.23 | convolution fusion | flops 12888047616 | bytes 8388616 | tf_op jit(solution)/shard_map/dot_general | solution.py:69
  201.4 18.0 %fusion.21 = f32[1024,1024]{1,0:T(8,128)} fusion(f32[1024,1024]{0,1:T(8,128)} %all-reduce.5.cloned.1.call-done, f32[]{:T(128)S(6)} %multiply.8, f32[1024,1024]{1,0:T(8,128)} %get-tuple-element.205, f32[]{:T(128)S(6)} %mul.38), kind=kOutput, calls=%fused_computation.31 | convolution fusion | flops 12886999040 | bytes 12582920 | tf_op jit(solution)/shard_map/dot_general | solution.py:54
  219.4 5.4 %copy.19 = f32[1024,1024]{0,1:T(8,128)} copy(f32[1024,1024]{1,0:T(8,128)} %fusion.21) | data formatting | bytes 8388608 | tf_op jit(solution)/shard_map/dot_general | solution.py:54
  224.7 27.6 %multiply_add_fusion = f32[1024,1024]{0,1:T(8,128)S(1)} fusion(f32[1024,1024]{0,1:T(8,128)} %copy.19, f32[1024,1024]{1,0:T(8,128)} %fusion.21, f32[1024,1024]{0,1:T(8,128)} %all-reduce.5.cloned.1.call-done, f32[]{:T(128)S(6)} %multiply.8, f32[1024,1024]{1,0:T(8,128)} %get-tuple-element.205, f32[]{:T(128)S(6)} %mul.38), kind=kOutput, calls=%fused_computation.22 | convolution fusion | flops 12892241920 | bytes 20971528 | tf_op jit(solution)/shard_map/dot_general | solution.py:55
  252.3 0.0 copy-start.1
  252.3 13.7 %fusion.22 = f32[1024,1024]{1,0:T(8,128)S(1)} fusion(f32[1024,1024]{0,1:T(8,128)S(1)} %multiply_add_fusion), kind=kOutput, calls=%fused_computation.36 | convolution fusion | flops 12884901888 | bytes 8388608 | tf_op jit(solution)/shard_map/dot_general | solution.py:69
  266.0 0.0 copy-done.1
  266.0 0.0 copy-start.2
  266.0 1.9 copy-done.2
  268.0 14.7 %fusion.23 = f32[1024,1024]{1,0:T(8,128)} fusion(f32[1024,1024]{0,1:T(8,128)S(1)} %multiply_add_fusion, f32[1024,1024]{1,0:T(8,128)S(1)} %fusion.22), kind=kOutput, calls=%fused_computation.37 | convolution fusion | flops 12884901888 | bytes 12582912 | tf_op jit(solution)/shard_map/dot_general | solution.py:54
  282.7 5.4 %copy.21 = f32[1024,1024]{0,1:T(8,128)} copy(f32[1024,1024]{1,0:T(8,128)} %fusion.23) | data formatting | bytes 8388608 | tf_op jit(solution)/shard_map/dot_general | solution.py:54
  288.1 19.3 %add_convert_fusion = bf16[1024,1024]{0,1:T(8,128)(2,1)S(1)} fusion(f32[1024,1024]{0,1:T(8,128)} %copy.21, f32[1024,1024]{0,1:T(8,128)} %copy-done.1, f32[1024,1024]{1,0:T(8,128)} %fusion.23, f32[1024,1024]{1,0:T(8,128)} %copy-done.2), kind=kOutput, calls=%fused_computation.21 | convolution fusion | flops 12891193344 | bytes 18874368 | tf_op jit(solution)/shard_map/dot_general | solution.py:55
  307.4 0.0 copy-start.3
  307.4 2.3 convolution_convert_fusion
  309.6 4.4 all-to-all-start
  314.0 0.0 copy-done.3
  314.0 0.6 convert_bitcast_fusion
  314.6 15.3 %all-to-all-done = bf16[512,8,128]{0,2,1:T(8,128)(2,1)S(1)} async-done(((bf16[512,8,128]{0,2,1:T(8,128)(2,1)}), bf16[512,8,128]{0,2,1:T(8,128)(2,1)S(1)}, u32[]{:S(2)}, u32[]{:S(2)}) %all-to-all-start) | async-done | bytes 1048608 | tf_op jit(solution)/shard_map/all_to_all | solution.py:75
  330.0 3.4 all-to-all-start.1
  333.3 0.0 all-reduce.7.cloned.1.call-start
  333.4 0.1 copy.34
  333.5 5.4 %all-to-all-done.1 = bf16[512,8,8]{0,2,1:T(8,128)(2,1)S(1)} async-done(((bf16[512,8,8]{0,2,1:T(8,128)(2,1)}), bf16[512,8,8]{0,2,1:T(8,128)(2,1)S(1)}, u32[]{:S(2)}, u32[]{:S(2)}) %all-to-all-start.1) | async-done | bytes 65568 | tf_op jit(solution)/shard_map/all_to_all | solution.py:76
  338.9 11.1 %while.28 = (s32[]{:T(128)}, f32[8,16,256]{2,1,0:T(8,128)S(1)}, f32[8,256]{1,0:T(8,128)S(1)}, bf16[4096,128]{0,1:T(8,128)(2,1)S(1)}, bf16[4096,8]{0,1:T(8,128)(2...) while((s32[]{:T(128)}, f32[8,16,256]{2,1,0:T(8,128)S(1)}, f32[8,256]{1,0:T(8,128)S(1)}, ...), condition=%wide.region_7.8_spmd.clone, body=%wide.region_5.7_spmd.clone.sunk | while | flops 155257088 | bytes 2000542 | solution.py:43
  338.9 2.9 fusion.48
  341.9 2.5 convert_reduce_fusion.2
  344.5 2.9 fusion.48
  347.4 2.5 convert_reduce_fusion.2
  350.0 0.6 copy-done.4
  350.7 0.0 all-reduce.7.cloned.1.call-update
  350.7 0.6 dynamic-slice
  351.9 2.3 copy.24
  354.2 39.1 %all-reduce.1 = f32[8,1,256]{2,0,1:T(8,128)S(1)} all-reduce(f32[8,1,256]{2,0,1:T(8,128)S(1)} %bitcast.64), channel_id=3, replica_groups=mesh['rows'=16,'sub'=8] {'rows'}, use_global_device_ids=true, to_apply=%region_9.10.clone | all-reduce | flops 2048 | bytes 16384
  393.4 0.1 dynamic-slice_bitcast_fusion.1
  393.4 36.8 %all-reduce.7.cloned.1.call-done = f32[8,16,256]{2,1,0:T(8,128)} async-done(((f32[8,16,256]{2,1,0:T(8,128)}), f32[8,16,256]{2,1,0:T(8,128)}) %all-reduce.7.cloned.1.call-update) | async-done | bytes 131088
  430.3 1.6 dynamic-slice_divide_fusion
  (21 shorter events, 0.3 us)
Async XLA Ops:
  7.2 9.9 %copy-start = (bf16[512,1024]{1,0:T(8,128)(2,1)S(1)}, bf16[512,1024]{1,0:T(8,128)(2,1)}, u32[]{:S(2)}) copy-start(bf16[512,1024]{1,0:T(8,128)(2,1)} %param.7) | copy-start | bytes 3145732
  7.2 169.9 %all-reduce.5.cloned.1.call-start = ((), (), s32[]{:S(2)}) async-start(), calls=%async_computation.2 | async-start | bytes 8388608 | tf_op jit(solution)/shard_map/psum | solution.py:65
  252.3 13.7 %copy-start.1 = (f32[1024,1024]{0,1:T(8,128)}, f32[1024,1024]{0,1:T(8,128)S(1)}, u32[]{:S(2)}) copy-start(f32[1024,1024]{0,1:T(8,128)S(1)} %multiply_add_fusion) | copy-start | bytes 12582916
  266.0 1.9 copy-start.2
  307.4 6.6 %copy-start.3 = (s32[512,64]{0,1:T(8,128)S(1)}, s32[512,64]{0,1:T(8,128)}, u32[]{:S(2)}) copy-start(s32[512,64]{0,1:T(8,128)} %param.8) | copy-start | bytes 393220
  309.6 20.3 %all-to-all-start = ((bf16[512,8,128]{0,2,1:T(8,128)(2,1)}), bf16[512,8,128]{0,2,1:T(8,128)(2,1)S(1)}, u32[]{:S(2)}, u32[]{:S(2)}) async-start(bf16[512,8,128]{0,2,1:T(8,128)(2,1)} %bitcast.3), calls=%async_computation | async-start | bytes 2097152 | tf_op jit(solution)/shard_map/all_to_all | solution.py:75
  330.0 8.9 %all-to-all-start.1 = ((bf16[512,8,8]{0,2,1:T(8,128)(2,1)}), bf16[512,8,8]{0,2,1:T(8,128)(2,1)S(1)}, u32[]{:S(2)}, u32[]{:S(2)}) async-start(bf16[512,8,8]{0,2,1:T(8,128)(2,1)} %convert_bitcast_fusion), calls=%async_computation.1 | async-start | bytes 131072 | tf_op jit(solution)/shard_map/all_to_all | solution.py:76
  333.3 97.0 %all-reduce.7.cloned.1.call-start = ((), (), s32[]{:S(2)}) async-start(), calls=%async_computation.3 | async-start | bytes 262144
  338.9 11.8 %copy-start.5 = (u32[128]{0:T(128)S(1)}, u32[128]{0:T(128)}, u32[]{:S(2)}) copy-start(u32[128]{0:T(128)} %constant.61) | copy-start | bytes 1540
  350.0 0.7 copy-start.4
Sparse Core Ops, SparseCore 0:
  20.5 156.5 all-reduce.4
  350.8 79.4 all-reduce.6
where the time goes:
time: 448 us; the launch traced here: 439 us
  waiting for transfers between devices  214 us (48%)
  matrix products  132 us (29%)
  blocking collectives  39.1 us (9%)
  local copies, waits for them, and re-layouts  17 us (4%)
  between operations  16.7 us (4%)
  other arithmetic  12.1 us (3%)
  starting transfers between devices  7.78 us (2%)
    psum x1, waiting for transfers between devices, per_device(): cross = lax.psum(local, ('rows', 'sub'))  157 us
    dot_general x2, matrix products, iterate(): jnp.dot(moved, gram, precision=highest)  46.9 us
    unnamed x1, blocking collectives  39.1 us
    unnamed x3, waiting for transfers between devices  36.9 us
    dot_general x2, matrix products, local_gram(): return lax.dot_general(current, current, contract, precision=highest)  32.8 us
    dot_general x2, matrix products, iterate(): moved = jnp.dot(polar, gram, precision=highest)  32.7 us
    all_to_all x1, waiting for transfers between devices, per_device(): lax.all_to_all(rotated, 'sub', split_axis=1, concat_axis=0, tiled=True)  15.3 us
    dot_general x2, local copies, waits for them, and re-layouts, iterate(): moved = jnp.dot(polar, gram, precision=highest)  10.7 us
  transfers between devices with their start and end apart: 4, of which 4 were waited for; matrix products, arithmetic and copies ran while one was open for 1% of the time, Pallas kernels for 0%

commit v1 on v0

--- a/solution.py
+++ b/solution.py
@@ -62,7 +62,7 @@
     highest = lax.Precision.HIGHEST
     contract = (((0,), (0,)), ((), ()))
     local = lax.dot_general(residuals, recon, contract, preferred_element_type=jnp.float32)
-    cross = lax.psum(local, ("rows", "sub"))
+    cross = lax.psum(lax.psum(local, "rows"), "sub")
     polar = cross / jnp.sqrt(jnp.sum(cross * cross) + 1e-06)
 
     def local_gram(current):

time: 448 us -> 473 us (1.056)
  waiting for transfers between devices: 214 us -> 239 us
    psum x1 -> x2, waiting for transfers between devices: 157 us -> 181 us  [per_device(): cross = lax.psum(lax.psum(local, 'rows'), 'sub')]
    unnamed x3 -> x4, waiting for transfers between devices: 36.9 us -> 37.3 us
  transfers between devices with their start and end apart: 4 -> 5, of which waited for: 4 -> 5; matrix products, arithmetic and copies ran while one was open for 1% -> 1% of each run, Pallas kernels for 0% -> 0%
where the time goes in v1:
time: 473 us; the launch traced here: 464 us
  waiting for transfers between devices  239 us (51%)
  matrix products  132 us (28%)
  blocking collectives  41 us (9%)
  local copies, waits for them, and re-layouts  17 us (4%)
  between operations  16.5 us (3%)
  other arithmetic  12.1 us (3%)
  starting transfers between devices  7.03 us (1%)
    psum x2, waiting for transfers between devices, per_device(): cross = lax.psum(lax.psum(local, 'rows'), 'sub')  181 us
    dot_general x2, matrix products, iterate(): jnp.dot(moved, gram, precision=highest)  46.9 us
    unnamed x1, blocking collectives  41 us
    unnamed x4, waiting for transfers between devices  37.3 us
    dot_general x2, matrix products, local_gram(): return lax.dot_general(current, current, contract, precision=highest)  32.8 us
    dot_general x2, matrix products, iterate(): moved = jnp.dot(polar, gram, precision=highest)  32.7 us
    all_to_all x1, waiting for transfers between devices, per_device(): lax.all_to_all(rotated, 'sub', split_axis=1, concat_axis=0, tiled=True)  15.2 us
    dot_general x2, local copies, waits for them, and re-layouts, iterate(): moved = jnp.dot(polar, gram, precision=highest)  10.7 us
  transfers between devices with their start and end apart: 5, of which 5 were waited for; matrix products, arithmetic and copies ran while one was open for 1% of the time, Pallas kernels for 0%

profile of v1, /device:TPU:0, one launch (start us, length us, event | category | flops | bytes accessed | tf_op | source)
XLA Modules:
  0.0 464.4 jit_solution(6452656530811824396)
XLA Ops:
  7.2 0.0 copy-start
  7.2 0.0 all-reduce.6.cloned.1.call-start
  7.2 1.0 convert_element_type.39
  8.2 8.8 %while.27 = (s32[]{:T(128)}, bf16[2,256,1024]{2,1,0:T(8,128)(2,1)S(1)}, bf16[2,256,64]{1,2,0:T(8,128)(2,1)S(1)}, bf16[64,16,256]{2,1,0:T(8,128)(2,1)}, s32[]{:T(128)}) while((s32[]{:T(128)}, bf16[2,256,1024]{2,1,0:T(8,128)(2,1)S(1)}, bf16[2,256,64]{1,2,0:T(8,128)(2,1)S(1)}, bf16[64,16,256]{2,1,0:T(8,128)(2,1)}, s32[]{:T(128)}) %tuple.72), condition=%wide.region_1.2_spmd.clone, body=%wide.region_0.1_spmd.clone.sunk | while | flops 138674432 | bytes 3245125 | solution.py:22
  8.3 4.1 fusion.45
  12.4 0.2 copy.38
  12.7 4.1 fusion.45
  16.8 0.2 copy.38
  17.1 0.0 copy-done
  17.1 3.2 convolution_bitcast_fusion
  20.3 0.0 all-reduce.6.cloned.1.call-update
  20.3 0.0 all-reduce.8.cloned.1.call-start
  20.4 106.2 %all-reduce.6.cloned.1.call-done = f32[1024,1024]{0,1:T(8,128)} async-done(((f32[1024,1024]{0,1:T(8,128)}), f32[1024,1024]{0,1:T(8,128)}) %all-reduce.6.cloned.1.call-update) | async-done | bytes 4194320 | tf_op jit(solution)/shard_map/psum | solution.py:65
  126.5 0.0 all-reduce.8.cloned.1.call-update
  126.6 74.6 %all-reduce.8.cloned.1.call-done = f32[1024,1024]{0,1:T(8,128)} async-done(((f32[1024,1024]{0,1:T(8,128)}), f32[1024,1024]{0,1:T(8,128)}) %all-reduce.8.cloned.1.call-update) | async-done | bytes 4194320 | tf_op jit(solution)/shard_map/psum | solution.py:65
  201.2 3.9 multiply_reduce_fusion.1
  205.8 19.1 %multiply_reduce_fusion = (f32[]{:T(128)}, f32[1024,1024]{1,0:T(8,128)}) fusion(f32[1024,1024]{0,1:T(8,128)} %all-reduce.8.cloned.1.call-done, f32[]{:T(128)S(6)} %sqrt.9), kind=kOutput, calls=%fused_computation.23 | convolution fusion | flops 12888047616 | bytes 8388616 | tf_op jit(solution)/shard_map/dot_general | solution.py:69
  225.6 18.0 %fusion.21 = f32[1024,1024]{1,0:T(8,128)} fusion(f32[1024,1024]{0,1:T(8,128)} %all-reduce.8.cloned.1.call-done, f32[]{:T(128)S(6)} %multiply.8, f32[1024,1024]{1,0:T(8,128)} %get-tuple-element.205, f32[]{:T(128)S(6)} %mul.38), kind=kOutput, calls=%fused_computation.31 | convolution fusion | flops 12886999040 | bytes 12582920 | tf_op jit(solution)/shard_map/dot_general | solution.py:54
  243.5 5.4 %copy.19 = f32[1024,1024]{0,1:T(8,128)} copy(f32[1024,1024]{1,0:T(8,128)} %fusion.21) | data formatting | bytes 8388608 | tf_op jit(solution)/shard_map/dot_general | solution.py:54
  248.9 27.6 %multiply_add_fusion = f32[1024,1024]{0,1:T(8,128)S(1)} fusion(f32[1024,1024]{0,1:T(8,128)} %copy.19, f32[1024,1024]{1,0:T(8,128)} %fusion.21, f32[1024,1024]{0,1:T(8,128)} %all-reduce.8.cloned.1.call-done, f32[]{:T(128)S(6)} %multiply.8, f32[1024,1024]{1,0:T(8,128)} %get-tuple-element.205, f32[]{:T(128)S(6)} %mul.38), kind=kOutput, calls=%fused_computation.22 | convolution fusion | flops 12892241920 | bytes 20971528 | tf_op jit(solution)/shard_map/dot_general | solution.py:55
  276.5 13.7 %fusion.22 = f32[1024,1024]{1,0:T(8,128)S(1)} fusion(f32[1024,1024]{0,1:T(8,128)S(1)} %multiply_add_fusion), kind=kOutput, calls=%fused_computation.36 | convolution fusion | flops 12884901888 | bytes 8388608 | tf_op jit(solution)/shard_map/dot_general | solution.py:69
  290.2 1.9 copy-done.2
  292.1 14.7 %fusion.23 = f32[1024,1024]{1,0:T(8,128)} fusion(f32[1024,1024]{0,1:T(8,128)S(1)} %multiply_add_fusion, f32[1024,1024]{1,0:T(8,128)S(1)} %fusion.22), kind=kOutput, calls=%fused_computation.37 | convolution fusion | flops 12884901888 | bytes 12582912 | tf_op jit(solution)/shard_map/dot_general | solution.py:54
  306.9 5.4 %copy.21 = f32[1024,1024]{0,1:T(8,128)} copy(f32[1024,1024]{1,0:T(8,128)} %fusion.23) | data formatting | bytes 8388608 | tf_op jit(solution)/shard_map/dot_general | solution.py:54
  312.2 19.3 %add_convert_fusion = bf16[1024,1024]{0,1:T(8,128)(2,1)S(1)} fusion(f32[1024,1024]{0,1:T(8,128)} %copy.21, f32[1024,1024]{0,1:T(8,128)} %copy-done.1, f32[1024,1024]{1,0:T(8,128)} %fusion.23, f32[1024,1024]{1,0:T(8,128)} %copy-done.2), kind=kOutput, calls=%fused_computation.21 | convolution fusion | flops 12891193344 | bytes 18874368 | tf_op jit(solution)/shard_map/dot_general | solution.py:55
  331.5 0.0 copy-start.3
  331.5 2.3 convolution_convert_fusion
  333.8 3.6 all-to-all-start
  337.4 0.0 copy-done.3
  337.4 0.6 convert_bitcast_fusion
  338.0 15.2 %all-to-all-done = bf16[512,8,128]{0,2,1:T(8,128)(2,1)S(1)} async-done(((bf16[512,8,128]{0,2,1:T(8,128)(2,1)}), bf16[512,8,128]{0,2,1:T(8,128)(2,1)S(1)}, u32[]{:S(2)}, u32[]{:S(2)}) %all-to-all-start) | async-done | bytes 1048608 | tf_op jit(solution)/shard_map/all_to_all | solution.py:75
  353.3 3.4 all-to-all-start.1
  356.6 0.0 all-reduce.10.cloned.1.call-start
  356.7 0.1 copy.34
  356.8 5.4 %all-to-all-done.1 = bf16[512,8,8]{0,2,1:T(8,128)(2,1)S(1)} async-done(((bf16[512,8,8]{0,2,1:T(8,128)(2,1)}), bf16[512,8,8]{0,2,1:T(8,128)(2,1)S(1)}, u32[]{:S(2)}, u32[]{:S(2)}) %all-to-all-start.1) | async-done | bytes 65568 | tf_op jit(solution)/shard_map/all_to_all | solution.py:76
  362.2 11.1 %while.28 = (s32[]{:T(128)}, f32[8,16,256]{2,1,0:T(8,128)S(1)}, f32[8,256]{1,0:T(8,128)S(1)}, bf16[4096,128]{0,1:T(8,128)(2,1)S(1)}, bf16[4096,8]{0,1:T(8,128)(2...) while((s32[]{:T(128)}, f32[8,16,256]{2,1,0:T(8,128)S(1)}, f32[8,256]{1,0:T(8,128)S(1)}, ...), condition=%wide.region_8.9_spmd.clone, body=%wide.region_6.8_spmd.clone.sunk | while | flops 155257088 | bytes 2000542 | solution.py:43
  362.2 2.9 fusion.48
  365.2 2.5 convert_reduce_fusion.2
  367.8 2.9 fusion.48
  370.7 2.5 convert_reduce_fusion.2
  373.3 0.6 copy-done.4
  374.0 0.0 all-reduce.10.cloned.1.call-update
  374.0 0.6 dynamic-slice
  375.2 2.3 copy.24
  377.5 41.0 %all-reduce.1 = f32[8,1,256]{2,0,1:T(8,128)S(1)} all-reduce(f32[8,1,256]{2,0,1:T(8,128)S(1)} %bitcast.64), channel_id=3, replica_groups=mesh['rows'=16,'sub'=8] {'rows'}, use_global_device_ids=true, to_apply=%region_10.11.clone | all-reduce | flops 2048 | bytes 16384
  418.5 0.1 dynamic-slice_bitcast_fusion.1
  418.6 37.3 %all-reduce.10.cloned.1.call-done = f32[8,16,256]{2,1,0:T(8,128)} async-done(((f32[8,16,256]{2,1,0:T(8,128)}), f32[8,16,256]{2,1,0:T(8,128)}) %all-reduce.10.cloned.1.call-update) | async-done | bytes 131088
  455.9 1.6 dynamic-slice_divide_fusion
  (24 shorter events, 0.3 us)
Async XLA Ops:
  7.2 9.9 %copy-start = (bf16[512,1024]{1,0:T(8,128)(2,1)S(1)}, bf16[512,1024]{1,0:T(8,128)(2,1)}, u32[]{:S(2)}) copy-start(bf16[512,1024]{1,0:T(8,128)(2,1)} %param.7) | copy-start | bytes 3145732
  7.2 119.4 %all-reduce.6.cloned.1.call-start = ((), (), s32[]{:S(2)}) async-start(), calls=%async_computation.2 | async-start | bytes 8388608 | tf_op jit(solution)/shard_map/psum | solution.py:65
  20.3 180.9 %all-reduce.8.cloned.1.call-start = ((), (), s32[]{:S(2)}) async-start(), calls=%async_computation.3 | async-start | bytes 8388608 | tf_op jit(solution)/shard_map/psum | solution.py:65
  276.5 13.7 %copy-start.1 = (f32[1024,1024]{0,1:T(8,128)}, f32[1024,1024]{0,1:T(8,128)S(1)}, u32[]{:S(2)}) copy-start(f32[1024,1024]{0,1:T(8,128)S(1)} %multiply_add_fusion) | copy-start | bytes 12582916
  290.2 1.9 copy-start.2
  331.5 5.8 %copy-start.3 = (s32[512,64]{0,1:T(8,128)S(1)}, s32[512,64]{0,1:T(8,128)}, u32[]{:S(2)}) copy-start(s32[512,64]{0,1:T(8,128)} %param.8) | copy-start | bytes 393220
  333.8 19.4 %all-to-all-start = ((bf16[512,8,128]{0,2,1:T(8,128)(2,1)}), bf16[512,8,128]{0,2,1:T(8,128)(2,1)S(1)}, u32[]{:S(2)}, u32[]{:S(2)}) async-start(bf16[512,8,128]{0,2,1:T(8,128)(2,1)} %bitcast.3), calls=%async_computation | async-start | bytes 2097152 | tf_op jit(solution)/shard_map/all_to_all | solution.py:75
  353.3 8.9 %all-to-all-start.1 = ((bf16[512,8,8]{0,2,1:T(8,128)(2,1)}), bf16[512,8,8]{0,2,1:T(8,128)(2,1)S(1)}, u32[]{:S(2)}, u32[]{:S(2)}) async-start(bf16[512,8,8]{0,2,1:T(8,128)(2,1)} %convert_bitcast_fusion), calls=%async_computation.1 | async-start | bytes 131072 | tf_op jit(solution)/shard_map/all_to_all | solution.py:76
  356.6 99.3 %all-reduce.10.cloned.1.call-start = ((), (), s32[]{:S(2)}) async-start(), calls=%async_computation.4 | async-start | bytes 262144
  362.2 11.8 %copy-start.5 = (u32[128]{0:T(128)S(1)}, u32[128]{0:T(128)}, u32[]{:S(2)}) copy-start(u32[128]{0:T(128)} %constant.61) | copy-start | bytes 1540
  373.3 0.7 copy-start.4
Sparse Core Ops, SparseCore 0:
  20.4 106.0 all-reduce.5
  128.9 72.2 all-reduce.7
  374.1 81.7 all-reduce.9
